TPU v7x, 512 devices: a whole 4x8x8 slice. The times are simulated.
512 devices in a mesh: ep: 64 (over y, x, core), tp: 8 (over z).
Axes of the slice: x: 4, y: 8, z: 8, core: 2. Of those that a mesh axis runs over, the one named last changes fastest.
Arguments:
- attn: bfloat16 [512, 4096], P('ep', 'tp'), may hold values from -6 to 6
- resid: bfloat16 [512, 4096], P('ep'), may hold values from -3 to 3
- wo: bfloat16 [4096, 4096], P('tp', 'ep'), may hold values from -0.09375 to 0.09375
- norm_gain: float32 [4096], replicated, may hold values from 0.25 to 1.75
- router: bfloat16 [4096, 8], replicated, may hold values from -0.09375 to 0.09375
- expert_ids: int32 [512, 2], P('ep'), may hold values from 0 to 7, all different within a row; in each aligned block of 8 rows (0 to 7, 8 to 15, ...) at most 4 rows name the same one
- w_gate: bfloat16 [4096, 65536], P(None, ('ep', 'tp')), may hold values from -0.09375 to 0.09375
- w_up: bfloat16 [4096, 65536], P(None, ('ep', 'tp')), may hold values from -0.09375 to 0.09375
- w_down: bfloat16 [65536, 4096], P(('ep', 'tp')), may hold values from -0.1875 to 0.1875
- lengths: int32 [64, 4], P('ep'), may hold values from 1 to 4, 8 in all within a row
- final_gain: float32 [4096], replicated, may hold values from 0.25 to 1.75
- head: bfloat16 [16384, 4096], P(('ep', 'tp')), may hold values from -0.375 to 0.375
Outputs:
- mixed: bfloat16 [512, 4096], P('ep')
- max_logit: float32 [256], replicated
Inputs may be any that keep to these rules, and one draw needn't show every extreme that they name: `expert_ids`: the two ids of a row differ; among the 8 rows of one index of ep no expert is named by more than 4 rows, a bound that some block reaches. Each row of lengths sums to 8, and its largest entry is 4.
All inputs are finite; a program needn't handle non-finite values.
Results may differ from a plain program's by a relative error of at most 0.0075.
Values may be sent and summed in bfloat16 or wider, within the bound.
A program may use at most 192 MiB of HBM per device.

v0:
```python
import jax
import jax.numpy as jnp
from jax import lax
from jax.sharding import PartitionSpec as P


def rms_scale(values, gain):
    return values * lax.rsqrt(jnp.mean(values * values, axis=1, keepdims=True) + 1e-05) * gain


def local(
    attn, resid, wo, norm_gain, router, expert_ids, w_gate, w_up, w_down, lengths, final_gain, head
):
    row_count = resid.shape[0]
    width = resid.shape[1]
    ep_count = lax.axis_size("ep")
    expert_count = router.shape[1]
    group_size = ep_count // expert_count
    capacity = row_count // 2
    partial_proj = jnp.dot(
        attn, lax.all_gather(wo, "ep", axis=1, tiled=True), preferred_element_type=jnp.float32
    )
    proj = lax.psum(partial_proj, "tp")
    stream = resid.astype(jnp.float32) + proj
    normed = rms_scale(stream, norm_gain).astype(jnp.bfloat16)
    logits = jnp.dot(normed, router, preferred_element_type=jnp.float32)
    expert_range = jnp.arange(expert_count, dtype=jnp.int32)
    one_hot = (expert_ids[:, :, None] == expert_range).astype(jnp.float32)
    picked = jnp.sum(one_hot * logits[:, None, :], axis=2)
    first = 1.0 / (1.0 + jnp.exp(picked[:, 1] - picked[:, 0]))
    second = 1.0 / (1.0 + jnp.exp(picked[:, 0] - picked[:, 1]))
    both_weights = jnp.stack([first, second], axis=1)
    flat_hot = (expert_ids.reshape(-1)[:, None] == expert_range).astype(jnp.int32)
    earlier = jnp.cumsum(flat_hot, axis=0) - flat_hot
    slot_index = jnp.sum(earlier * flat_hot, axis=1)
    target = (expert_ids.reshape(-1) * capacity + slot_index).reshape(row_count, 2)
    slot_range = jnp.arange(expert_count * capacity, dtype=jnp.int32)
    placed = (target[:, :, None] == slot_range).astype(jnp.float32)
    dispatch_matrix = jnp.sum(placed, axis=1).astype(jnp.bfloat16)
    combine_matrix = jnp.sum(placed * both_weights[:, :, None], axis=1)
    send_rows = lax.dot_general(
        dispatch_matrix, normed, (((0,), (0,)), ((), ())), preferred_element_type=jnp.float32
    ).astype(jnp.bfloat16)
    per_expert = send_rows.reshape(expert_count, 1, capacity, width)
    outgoing = jnp.broadcast_to(per_expert, (expert_count, group_size, capacity, width))
    outgoing = outgoing.reshape(ep_count, capacity, width)
    arrived = lax.all_to_all(outgoing, "ep", split_axis=0, concat_axis=0, tiled=True)
    flat_rows = arrived.reshape(-1, width)
    gate = jnp.dot(flat_rows, w_gate, preferred_element_type=jnp.float32)
    upper = jnp.dot(flat_rows, w_up, preferred_element_type=jnp.float32)
    hidden = (jax.nn.silu(gate) * upper).astype(jnp.bfloat16)
    term = jnp.dot(hidden, w_down, preferred_element_type=jnp.float32).astype(jnp.bfloat16)
    term = term.reshape(arrived.shape[0], arrived.shape[1], width)
    returned = lax.all_to_all(term, "ep", split_axis=0, concat_axis=0, tiled=True)
    back_width = returned.shape[2]
    grouped = returned.reshape(expert_count, group_size, capacity, back_width).astype(jnp.float32)
    grouped = jnp.sum(grouped, axis=1).reshape(expert_count * capacity, back_width)
    expert_part = jnp.dot(
        combine_matrix, grouped, precision=lax.Precision.HIGHEST, preferred_element_type=jnp.float32
    )
    expert_total = lax.psum(expert_part, "tp")
    mixed = (stream + expert_total).astype(jnp.bfloat16)
    ends = jnp.cumsum(lengths[0]) - 1
    row_range = jnp.arange(row_count, dtype=jnp.int32)
    selector = (ends[:, None] == row_range).astype(jnp.bfloat16)
    last = jnp.dot(selector, mixed, preferred_element_type=jnp.float32)
    final = rms_scale(last, final_gain).astype(jnp.bfloat16)
    vocab_logits = lax.dot_general(
        lax.all_gather(final, "ep", axis=0, tiled=True),
        head,
        (((1,), (1,)), ((), ())),
        preferred_element_type=jnp.float32,
    )
    local_max = jnp.max(vocab_logits, axis=1)
    max_logit = lax.pmax(local_max, ("ep", "tp"))
    return (mixed, max_logit)


def solution(mesh):
    placed = (
        P("ep", "tp"),
        P("ep", None),
        P("tp", "ep"),
        P(),
        P(),
        P("ep", None),
        P(None, ("ep", "tp")),
        P(None, ("ep", "tp")),
        P(("ep", "tp"), None),
        P("ep", None),
        P(),
        P(("ep", "tp"), None),
    )
    return jax.shard_map(
        local, mesh=mesh, in_specs=placed, out_specs=(P("ep", None), P()), check_vma=False
    )
```

profile of v0, /device:TPU:1, one launch (start us, length us, event | category | flops | bytes accessed | tf_op | source)
XLA Modules:
  0.0 583.7 jit_solution(15072324507917972072)
XLA Ops:
  7.2 0.7 all-gather.4.cloned.1.call-update
  8.0 0.8 copy.24
  8.9 0.2 select_reduce_fusion.2
  9.2 92.4 %all-gather.4.cloned.1.call-done = bf16[512,4096]{0,1:T(8,128)(2,1)} async-done(((bf16[512,64]{0,1:T(8,128)(2,1)}), bf16[512,4096]{0,1:T(8,128)(2,1)}) %all-gather.4.cloned.1.call-update) | async-done | bytes 4194320 | tf_op jit(solution)/shard_map/all_gather | solution.py:21
  101.6 4.0 fusion.13
  105.7 71.1 %all-reduce.3.cloned.1.call-done = f32[8,4096]{1,0:T(8,128)} async-done(((f32[8,4096]{1,0:T(8,128)}), f32[8,4096]{1,0:T(8,128)}) %all-reduce.3.cloned.1.call-update) | async-done | bytes 131088 | tf_op jit(solution)/shard_map/psum | solution.py:23
  176.8 1.1 multiply_reduce_fusion
  177.9 1.0 multiply_convert_fusion
  178.9 0.1 fusion.14
  179.0 0.2 select_reduce_fusion.1
  179.3 0.3 convolution_convert_fusion.1
  179.6 0.1 broadcast_in_dim.4
  179.7 1.0 broadcast_in_dim.5
  180.7 64.7 %all_to_all.10 = bf16[64,4,4096]{2,1,0:T(4,128)(2,1)} all-to-all(bf16[64,4,4096]{2,1,0:T(4,128)(2,1)S(1)} %bitcast.25), channel_id=1, replica_groups=mesh['ep'=64,'tp'=8] {'ep'}, dimensions={0} | all-to-all | bytes 4194304 | tf_op jit(solution)/shard_map/all_to_all | solution.py:47
  245.4 2.5 reshape.76
  248.0 1.9 fusion.15
  249.9 3.9 convolution_convert_fusion
  253.8 4.1 reshape.77
  257.9 7.1 %all-to-all-start.1 = ((bf16[64,4,4096]{2,1,0:T(4,128)(2,1)}), bf16[64,4,4096]{2,1,0:T(4,128)(2,1)S(1)}, u32[]{:S(2)}, u32[]{:S(2)}) async-start(bf16[64,4,4096]{2,1,0:T(4,128)(2,1)} %reshape.77), calls=%async_computation.1 | async-start | bytes 4194304 | tf_op jit(solution)/shard_map/all_to_all | solution.py:54
  265.1 0.2 reduce-window.8
  265.3 49.5 %all-to-all-done.1 = bf16[64,4,4096]{2,1,0:T(4,128)(2,1)S(1)} async-done(((bf16[64,4,4096]{2,1,0:T(4,128)(2,1)}), bf16[64,4,4096]{2,1,0:T(4,128)(2,1)S(1)}, u32[]{:S(2)}, u32[]{:S(2)}) %all-to-all-start.1) | async-done | bytes 2097184 | tf_op jit(solution)/shard_map/all_to_all | solution.py:54
  314.7 1.9 convert_reduce_fusion
  316.6 1.2 reshape.78
  317.8 1.0 fusion.16
  318.9 68.8 %all-reduce.5.cloned.1.call-done = f32[8,4096]{1,0:T(8,128)} async-done(((f32[8,4096]{1,0:T(8,128)}), f32[8,4096]{1,0:T(8,128)}) %all-reduce.5.cloned.1.call-update) | async-done | bytes 131088 | tf_op jit(solution)/shard_map/psum | solution.py:61
  387.7 0.9 add_convert_fusion
  388.7 0.3 multiply_reduce_fusion.1
  389.0 0.7 fusion.7
  389.7 87.1 %all-gather.6.cloned.1.call-done = bf16[64,4,4096]{2,1,0:T(4,128)(2,1)} async-done(((bf16[1,4,4096]{2,1,0:T(4,128)(2,1)}), bf16[64,4,4096]{2,1,0:T(4,128)(2,1)}) %all-gather.6.cloned.1.call-update) | async-done | bytes 2097168 | tf_op jit(solution)/shard_map/all_gather | solution.py:69
  476.8 2.5 reshape.82
  479.4 0.8 convolution_reduce_fusion
  480.1 97.0 %pmax.7 = f32[256]{0:T(256)} all-reduce(f32[256]{0:T(256)S(1)} %convolution_reduce_fusion), channel_id=1, replica_groups=mesh['ep'=64,'tp'=8] {'ep','tp'}, use_global_device_ids=true, to_apply=%region_12.13 | all-reduce | flops 256 | bytes 2048 | tf_op jit(solution)/shard_map/pmax | solution.py:75
  (39 shorter events, 0.7 us)
Async XLA Ops:
  7.2 242.7 %copy-start = (bf16[128,4096]{1,0:T(8,128)(2,1)S(1)}, bf16[128,4096]{1,0:T(8,128)(2,1)}, u32[]{:S(2)}) copy-start(bf16[128,4096]{1,0:T(8,128)(2,1)} %param.20) | copy-start | bytes 3145732
  7.2 94.4 %all-gather.4.cloned.1.call-start = ((), (), s32[]{:S(2)}) async-start(), calls=%async_computation.2 | async-start | bytes 4259840 | tf_op jit(solution)/shard_map/all_gather | solution.py:21
  7.9 168.9 %all-reduce.3.cloned.1.call-start = ((), (), s32[]{:S(2)}) async-start(), calls=%async_computation.3 | async-start | bytes 262144 | tf_op jit(solution)/shard_map/psum | solution.py:23
  9.2 167.6 %copy-start.2 = (bf16[8,4096]{1,0:T(8,128)(2,1)S(1)}, bf16[8,4096]{1,0:T(8,128)(2,1)}, u32[]{:S(2)}) copy-start(bf16[8,4096]{1,0:T(8,128)(2,1)} %param.13) | copy-start | bytes 196612
  9.2 168.7 %copy-start.6 = (f32[4096]{0:T(1024)S(1)}, f32[4096]{0:T(1024)}, u32[]{:S(2)}) copy-start(f32[4096]{0:T(1024)} %param.15) | copy-start | bytes 49156
  9.2 169.7 %copy-start.5 = (bf16[4096,8]{0,1:T(8,128)(2,1)S(1)}, bf16[4096,8]{0,1:T(8,128)(2,1)}, u32[]{:S(2)}) copy-start(bf16[4096,8]{0,1:T(8,128)(2,1)} %param.16) | copy-start | bytes 196612
  9.2 169.8 %copy-start.8 = (s32[8,2]{0,1:T(2,128)S(1)}, s32[8,2]{0,1:T(2,128)}, u32[]{:S(2)}) copy-start(s32[8,2]{0,1:T(2,128)} %param.17) | copy-start | bytes 196
  257.9 7.2 %copy-start.9 = (s32[1,4]{1,0:T(1,128)S(1)}, s32[1,4]{1,0:T(1,128)}, u32[]{:S(2)}) copy-start(s32[1,4]{1,0:T(1,128)} %param.21) | copy-start | bytes 52
  257.9 56.8 %all-to-all-start.1 = ((bf16[64,4,4096]{2,1,0:T(4,128)(2,1)}), bf16[64,4,4096]{2,1,0:T(4,128)(2,1)S(1)}, u32[]{:S(2)}, u32[]{:S(2)}) async-start(bf16[64,4,4096]{2,1,0:T(4,128)(2,1)} %reshape.77), calls=%async_computation.1 | async-start | bytes 4194304 | tf_op jit(solution)/shard_map/all_to_all | solution.py:54
  265.0 122.7 %all-reduce.5.cloned.1.call-start = ((), (), s32[]{:S(2)}) async-start(), calls=%async_computation.4 | async-start | bytes 262144 | tf_op jit(solution)/shard_map/psum | solution.py:61
  265.3 122.4 %copy-start.1 = (f32[8,4096]{1,0:T(8,128)S(1)}, f32[8,4096]{1,0:T(8,128)}, u32[]{:S(2)}) copy-start(f32[8,4096]{1,0:T(8,128)} %all-reduce.3.cloned.1.call-done) | copy-start | bytes 393220
  265.3 123.7 %copy-start.7 = (f32[4096]{0:T(1024)S(1)}, f32[4096]{0:T(1024)}, u32[]{:S(2)}) copy-start(f32[4096]{0:T(1024)} %param.22) | copy-start | bytes 49156
  318.9 157.9 %all-gather.6.cloned.1.call-start = ((), (), s32[]{:S(2)}) async-start(), calls=%async_computation.5 | async-start | bytes 2129920 | tf_op jit(solution)/shard_map/all_gather | solution.py:69
  388.6 90.7 %copy-start.4 = (bf16[8,4096]{1,0:T(8,128)(2,1)}, bf16[8,4096]{1,0:T(8,128)(2,1)S(1)}, u32[]{:S(2)}) copy-start(bf16[8,4096]{1,0:T(8,128)(2,1)S(1)} %add_convert_fusion) | copy-start | bytes 196612
  389.7 89.6 %copy-start.3 = (bf16[32,4096]{1,0:T(8,128)(2,1)S(1)}, bf16[32,4096]{1,0:T(8,128)(2,1)}, u32[]{:S(2)}) copy-start(bf16[32,4096]{1,0:T(8,128)(2,1)} %param.23) | copy-start | bytes 786436
Sparse Core Ops, SparseCore 0:
  11.3 90.1 all-gather.3
  105.7 71.0 all-reduce.2
  319.0 68.6 all-reduce.4
  390.9 85.8 all-gather.5
where the time goes:
time: 584 us
  waiting for transfers between devices  369 us (63%)
  blocking collectives  162 us (28%)
  between operations  14 us (2%)
  local copies, waits for them, and re-layouts  12.6 us (2%)
  matrix products  12.4 us (2%)
  starting transfers between devices  7.25 us (1%)
  other arithmetic  6.28 us (1%)
    pmax x1, blocking collectives, local(): max_logit = lax.pmax(local_max, ('ep', 'tp'))  97 us
    all_gather x1, waiting for transfers between devices, local(): lax.all_gather(wo, 'ep', axis=1, tiled=True)  92.4 us
    all_gather x1, waiting for transfers between devices, local(): lax.all_gather(final, 'ep', axis=0, tiled=True)  87.1 us
    psum x1, waiting for transfers between devices, local(): proj = lax.psum(partial_proj, 'tp')  71.1 us
    psum x1, waiting for transfers between devices, local(): expert_total = lax.psum(expert_part, 'tp')  68.8 us
    all_to_all x1, blocking collectives, local(): lax.all_to_all(outgoing, 'ep', split_axis=0, concat_axis=0, tiled=True)  64.7 us
    all_to_all x1, waiting for transfers between devices, local(): lax.all_to_all(term, 'ep', split_axis=0, concat_axis=0, tiled=True)  49.5 us
  transfers between devices with their start and end apart: 5, of which 5 were waited for; matrix products, arithmetic and copies ran while one was open for 0% of the time, Pallas kernels for 0%

commit v1 on v0

--- a/solution.py
+++ b/solution.py
@@ -58,7 +58,7 @@
     expert_part = jnp.dot(
         combine_matrix, grouped, precision=lax.Precision.HIGHEST, preferred_element_type=jnp.float32
     )
-    expert_total = lax.psum(expert_part, "tp")
+    expert_total = jnp.sum(lax.all_gather(expert_part, "tp"), axis=0)
     mixed = (stream + expert_total).astype(jnp.bfloat16)
     ends = jnp.cumsum(lengths[0]) - 1
     row_range = jnp.arange(row_count, dtype=jnp.int32)

time: 584 us -> 544 us (0.932)
  waiting for transfers between devices: 369 us -> 283 us
  blocking collectives: 162 us -> 218 us
  starting transfers between devices: 7.25 us -> 0.16 us
    psum x1 -> x0, waiting for transfers between devices: 68.8 us -> none  [local(): expert_total = lax.psum(expert_part, 'tp')]
    all_to_all x0 -> x1, blocking collectives: none -> 56.5 us  [local(): lax.all_to_all(term, 'ep', split_axis=0, concat_axis=0, tiled=True)]
    all_to_all x1 -> x0, waiting for transfers between devices: 49.5 us -> none  [local(): lax.all_to_all(term, 'ep', split_axis=0, concat_axis=0, tiled=True)]
    all_gather x0 -> x1, waiting for transfers between devices: none -> 31.9 us  [local(): expert_total = jnp.sum(lax.all_gather(expert_part, 'tp'), axis=0)]
    all_to_all x1 -> x0, starting transfers between devices: 7.09 us -> none  [local(): lax.all_to_all(term, 'ep', split_axis=0, concat_axis=0, tiled=True)]
  transfers between devices with their start and end apart: 5 -> 4, of which waited for: 5 -> 4; matrix products, arithmetic and copies ran while one was open for 0% -> 0% of each run, Pallas kernels for 0% -> 0%
where the time goes in v1:
time: 544 us; the launch traced here: 543 us
  waiting for transfers between devices  283 us (52%)
  blocking collectives  218 us (40%)
  between operations  14 us (3%)
  matrix products  12.4 us (2%)
  local copies, waits for them, and re-layouts  10.2 us (2%)
  other arithmetic  5.9 us (1%)
    pmax x1, blocking collectives, local(): max_logit = lax.pmax(local_max, ('ep', 'tp'))  97 us
    all_gather x1, waiting for transfers between devices, local(): lax.all_gather(wo, 'ep', axis=1, tiled=True)  92.4 us
    all_gather x1, waiting for transfers between devices, local(): lax.all_gather(final, 'ep', axis=0, tiled=True)  86.5 us
    psum x1, waiting for transfers between devices, local(): proj = lax.psum(partial_proj, 'tp')  71 us
    all_to_all x1, blocking collectives, local(): lax.all_to_all(outgoing, 'ep', split_axis=0, concat_axis=0, tiled=True)  64.7 us
    all_to_all x1, blocking collectives, local(): lax.all_to_all(term, 'ep', split_axis=0, concat_axis=0, tiled=True)  56.5 us
    all_gather x1, waiting for transfers between devices, local(): expert_total = jnp.sum(lax.all_gather(expert_part, 'tp'), axis=0)  31.9 us
  transfers between devices with their start and end apart: 4, of which 4 were waited for; matrix products, arithmetic and copies ran while one was open for 0% of the time, Pallas kernels for 0%

profile of v1, /device:TPU:1, one launch (start us, length us, event | category | flops | bytes accessed | tf_op | source)
XLA Modules:
  0.0 543.3 jit_solution(13214055922841127720)
XLA Ops:
  7.2 0.7 all-gather.6.cloned.1.call-update
  8.0 0.8 copy.24
  8.9 0.2 select_reduce_fusion.2
  9.2 92.4 %all-gather.6.cloned.1.call-done = bf16[512,4096]{0,1:T(8,128)(2,1)} async-done(((bf16[512,64]{0,1:T(8,128)(2,1)}), bf16[512,4096]{0,1:T(8,128)(2,1)}) %all-gather.6.cloned.1.call-update) | async-done | bytes 4194320 | tf_op jit(solution)/shard_map/all_gather | solution.py:21
  101.6 4.0 fusion.13
  105.7 0.1 copy.26
  105.8 71.0 %all-reduce.2.cloned.1.call-done = f32[8,4096]{1,0:T(8,128)} async-done(((f32[8,4096]{1,0:T(8,128)}), f32[8,4096]{1,0:T(8,128)}) %all-reduce.2.cloned.1.call-update) | async-done | bytes 131088 | tf_op jit(solution)/shard_map/psum | solution.py:23
  176.8 1.1 multiply_reduce_fusion
  177.9 1.0 multiply_convert_fusion
  178.9 0.1 fusion.14
  179.0 0.2 select_reduce_fusion.1
  179.3 0.3 convolution_convert_fusion.1
  179.6 0.1 broadcast_in_dim.4
  179.7 1.0 broadcast_in_dim.5
  180.7 64.7 %all_to_all.10 = bf16[64,4,4096]{2,1,0:T(4,128)(2,1)} all-to-all(bf16[64,4,4096]{2,1,0:T(4,128)(2,1)S(1)} %bitcast.27), channel_id=1, replica_groups=mesh['ep'=64,'tp'=8] {'ep'}, dimensions={0} | all-to-all | bytes 4194304 | tf_op jit(solution)/shard_map/all_to_all | solution.py:47
  245.4 2.5 reshape.76
  248.0 1.9 fusion.15
  249.9 3.9 convolution_convert_fusion
  253.8 2.7 reshape.77
  256.6 56.5 %all_to_all.11 = bf16[64,4,4096]{2,1,0:T(4,128)(2,1)S(1)} all-to-all(bf16[64,4,4096]{2,1,0:T(4,128)(2,1)S(1)} %reshape.77), channel_id=1, replica_groups=mesh['ep'=64,'tp'=8] {'ep'}, dimensions={0} | all-to-all | bytes 4194304 | tf_op jit(solution)/shard_map/all_to_all | solution.py:54
  313.0 1.1 convert_reduce_fusion
  314.2 0.2 reshape.78
  314.3 1.0 fusion.16
  315.4 0.2 reduce-window.8
  315.6 31.9 %all-gather.8.cloned.1.call-done = f32[64,4096]{1,0:T(8,128)} async-done(((f32[8,4096]{1,0:T(8,128)}), f32[64,4096]{1,0:T(8,128)}) %all-gather.8.cloned.1.call-update) | async-done | bytes 1048592 | tf_op jit(solution)/shard_map/all_gather | solution.py:61
  347.5 1.3 bitcast_reduce_fusion
  348.8 0.3 multiply_reduce_fusion.1
  349.2 0.7 fusion.7
  349.9 86.5 %all-gather.10.cloned.1.call-done = bf16[64,4,4096]{2,1,0:T(4,128)(2,1)} async-done(((bf16[1,4,4096]{2,1,0:T(4,128)(2,1)}), bf16[64,4,4096]{2,1,0:T(4,128)(2,1)}) %all-gather.10.cloned.1.call-update) | async-done | bytes 2097168 | tf_op jit(solution)/shard_map/all_gather | solution.py:69
  436.5 2.5 reshape.83
  439.0 0.8 convolution_reduce_fusion
  439.8 97.0 %pmax.7 = f32[256]{0:T(256)} all-reduce(f32[256]{0:T(256)S(1)} %convolution_reduce_fusion), channel_id=1, replica_groups=mesh['ep'=64,'tp'=8] {'ep','tp'}, use_global_device_ids=true, to_apply=%region_12.13 | all-reduce | flops 256 | bytes 2048 | tf_op jit(solution)/shard_map/pmax | solution.py:75
  (39 shorter events, 0.7 us)
Async XLA Ops:
  7.2 242.7 %copy-start = (bf16[128,4096]{1,0:T(8,128)(2,1)S(1)}, bf16[128,4096]{1,0:T(8,128)(2,1)}, u32[]{:S(2)}) copy-start(bf16[128,4096]{1,0:T(8,128)(2,1)} %param.20) | copy-start | bytes 3145732
  7.2 94.4 %all-gather.6.cloned.1.call-start = ((), (), s32[]{:S(2)}) async-start(), calls=%async_computation.2 | async-start | bytes 4259840 | tf_op jit(solution)/shard_map/all_gather | solution.py:21
  7.9 168.9 %all-reduce.2.cloned.1.call-start = ((), (), s32[]{:S(2)}) async-start(), calls=%async_computation.3 | async-start | bytes 262144 | tf_op jit(solution)/shard_map/psum | solution.py:23
  9.2 167.6 %copy-start.2 = (bf16[8,4096]{1,0:T(8,128)(2,1)S(1)}, bf16[8,4096]{1,0:T(8,128)(2,1)}, u32[]{:S(2)}) copy-start(bf16[8,4096]{1,0:T(8,128)(2,1)} %param.13) | copy-start | bytes 196612
  9.2 168.7 %copy-start.6 = (f32[4096]{0:T(1024)S(1)}, f32[4096]{0:T(1024)}, u32[]{:S(2)}) copy-start(f32[4096]{0:T(1024)} %param.15) | copy-start | bytes 49156
  9.2 169.7 %copy-start.5 = (bf16[4096,8]{0,1:T(8,128)(2,1)S(1)}, bf16[4096,8]{0,1:T(8,128)(2,1)}, u32[]{:S(2)}) copy-start(bf16[4096,8]{0,1:T(8,128)(2,1)} %param.16) | copy-start | bytes 196612
  9.2 169.8 %copy-start.8 = (s32[8,2]{0,1:T(2,128)S(1)}, s32[8,2]{0,1:T(2,128)}, u32[]{:S(2)}) copy-start(s32[8,2]{0,1:T(2,128)} %param.17) | copy-start | bytes 196
  105.6 241.9 %all-gather.8.cloned.1.call-start = ((), (), s32[]{:S(2)}) async-start(), calls=%async_computation.4 | async-start | bytes 1179648 | tf_op jit(solution)/shard_map/all_gather | solution.py:61
  313.0 2.4 copy-start.9
  314.1 34.6 %copy-start.1 = (f32[8,4096]{1,0:T(8,128)S(1)}, f32[8,4096]{1,0:T(8,128)}, u32[]{:S(2)}) copy-start(f32[8,4096]{1,0:T(8,128)} %all-reduce.2.cloned.1.call-done) | copy-start | bytes 393220
  314.1 35.0 %copy-start.7 = (f32[4096]{0:T(1024)S(1)}, f32[4096]{0:T(1024)}, u32[]{:S(2)}) copy-start(f32[4096]{0:T(1024)} %param.22) | copy-start | bytes 49156
  315.4 121.1 %all-gather.10.cloned.1.call-start = ((), (), s32[]{:S(2)}) async-start(), calls=%async_computation.5 | async-start | bytes 2129920 | tf_op jit(solution)/shard_map/all_gather | solution.py:69
  348.8 90.2 %copy-start.4 = (bf16[8,4096]{1,0:T(8,128)(2,1)}, bf16[8,4096]{1,0:T(8,128)(2,1)S(1)}, u32[]{:S(2)}) copy-start(bf16[8,4096]{1,0:T(8,128)(2,1)S(1)} %add_convert_fusion) | copy-start | bytes 196612
  349.9 89.1 %copy-start.3 = (bf16[32,4096]{1,0:T(8,128)(2,1)S(1)}, bf16[32,4096]{1,0:T(8,128)(2,1)}, u32[]{:S(2)}) copy-start(bf16[32,4096]{1,0:T(8,128)(2,1)} %param.23) | copy-start | bytes 786436
Sparse Core Ops, SparseCore 0:
  11.3 90.1 all-gather.5
  105.7 71.0 all-reduce.1
  315.5 31.9 all-gather.7
  350.7 85.7 all-gather.9
